TPU v7x, 128 devices: a whole 4x4x4 slice. The times are simulated.
128 devices in a mesh: grp: 4 (over x), row: 32 (over z, y, core).
Axes of the slice: x: 4, y: 4, z: 4, core: 2. Of those that a mesh axis runs over, the one named last changes fastest.
Arguments:
- snapshots: bfloat16 [8192, 131072], P(None, ('grp', 'row')), may hold values from -8 to 8
- weights: float32 [131072], P(('grp', 'row')), may hold values from 0.25 to 4
- reference_field: float32 [131072], P(('grp', 'row')), may hold values from -6 to 6
- start_basis: float32 [64, 2, 63, 8], replicated, may hold values from -6 to 6
Outputs:
- spod_modes: float32 [64, 16, 131072], P(None, None, ('grp', 'row'))
- energies: float32 [64, 8], replicated
All inputs are finite; a program needn't handle non-finite values.
Results may differ from a plain program's by a relative error of at most 0.012.
The roundings to bfloat16 on the way count: a program that leaves them out, or rounds other values in their place, can miss the bound.
Values may be sent and summed in bfloat16 or wider, within the bound.
A program may use at most 192 MiB of HBM per device.

v0:
```python
import functools
import math

import numpy as np
import jax
import jax.numpy as jnp
from jax import lax
from jax.experimental import pallas as pl
from jax.experimental.pallas import tpu as pltpu
from jax.sharding import PartitionSpec as P

NFFT = 256
NBLK = 63
NF = 64
NM = 8
ITERS = 12
XC = 256
MESH = pl.DeviceIdType.MESH


def dft_table():
    steps = np.arange(NFFT, dtype=np.int32)
    bins = np.arange(1, NF + 1, dtype=np.int32)
    wrapped = bins[:, None] * steps[None, :] % NFFT
    angles = np.float32(2.0 * math.pi / NFFT) * wrapped.astype(np.float32)
    taper = np.float32(0.5) - np.float32(0.5) * np.cos(
        np.float32(2.0 * math.pi / NFFT) * steps.astype(np.float32)
    )
    scaled = taper / np.sqrt(np.sum(taper * taper))
    stacked = np.stack([np.cos(angles), -np.sin(angles)]) * scaled[None, None, :]
    return stacked.astype(jnp.bfloat16)


def pair_tables():
    rows = dft_table().reshape(2 * NF, NFFT)
    tables = np.zeros((8, 256, 384), rows.dtype)
    for r in range(8):
        for g in range(16):
            for w in range(8):
                source = rows[8 * g + (w - r) % 8]
                tables[r, 16 * g + 2 * w, :256] = source
                tables[r, 16 * g + 2 * w + 1, 128:] = source
    return tables


def packed_masks():
    row = lax.broadcasted_iota(jnp.int32, (64, 128), 0)
    lane = lax.broadcasted_iota(jnp.int32, (64, 128), 1)
    left = lane < 64
    return left, jnp.where(left, 1.0, -1.0), row <= lane % 64


def transform_kernel(
    total_rows, devices, inner,
    snap_ref, table_ref, weight_ref, field_ref, start_ref,
    coeff_ref, share_ref,
    buf, stage, gram_ref, slots, snap_sems, sum_send, sum_recv, share_send, share_recv,
):
    pieces = 4
    piece_rows = snap_ref.shape[0] // pieces
    chunks = snap_ref.shape[1] // XC
    rows = snap_ref.shape[0]
    grp, row = lax.axis_index("grp"), lax.axis_index("row")
    me = grp * inner + row
    mine = me // 2
    is_owner = row % 2 == mine % 2

    def device(index):
        return (index // inner, index % inner)

    barrier = pltpu.get_barrier_semaphore()

    def greet(k, carry):
        pl.semaphore_signal(barrier, inc=1, device_id=device((me + k) % devices), device_id_type=MESH)
        return carry

    def piece_copy(chunk, slot, piece):
        lanes = pl.ds(pl.multiple_of(chunk * XC, XC), XC)
        span = pl.ds(piece * piece_rows, piece_rows)
        return pltpu.make_async_copy(
            snap_ref.at[span, lanes], buf.at[slot, span, :], snap_sems.at[slot, piece]
        )

    for piece in range(pieces):
        piece_copy(0, 0, piece).start()
    lax.fori_loop(1, devices, greet, 0)
    for slot in range(2):
        buf[slot, rows:, :] = jnp.zeros((128, XC), jnp.bfloat16)
    word = lax.broadcasted_iota(jnp.int32, (16, XC), 0) // 2
    odd_row = lax.broadcasted_iota(jnp.int32, (256, XC), 0)
    is_odd = odd_row % 2 == 1
    real_half = odd_row < 128
    bits = [(word // s) % 2 == 1 for s in (1, 2, 4)]

    def step(s, carry):
        chunk, group = s // 4, s % 4
        slot = chunk % 2
        lanes = pl.ds(pl.multiple_of(chunk * XC, XC), XC)

        @pl.when(jnp.logical_and(group == 0, chunk + 1 < chunks))
        def _():
            for piece in range(pieces):
                piece_copy(chunk + 1, 1 - slot, piece).start()

        @pl.when(group == 0)
        def _():
            piece_copy(chunk, slot, 0).wait()
            piece_copy(chunk, slot, 1).wait()

        @pl.when(group == 1)
        def _():
            piece_copy(chunk, slot, 2).wait()

        @pl.when(group == 2)
        def _():
            piece_copy(chunk, slot, 3).wait()

        root = jnp.sqrt(weight_ref[:, lanes])
        for r in range(8):
            first = pl.multiple_of((group * 8 + r) * 256, 256)
            out = jnp.dot(
                table_ref[r], buf[slot, pl.ds(first, 384), :], preferred_element_type=jnp.float32
            )
            out = out * root
            if r == 7:
                probe = jnp.where(real_half, root * field_ref[:, lanes], 0.0)
                out = jnp.where(jnp.logical_and(is_odd, group == 3), probe, out)
            stage[r] = out.astype(jnp.bfloat16)
        for g in range(16):
            tiles = [stage[r, 16 * g : 16 * g + 16, :] for r in range(8)]
            for level, bit in zip((1, 2, 4), bits):
                tiles = [jnp.where(bit, tiles[(m + level) % 8], tiles[m]) for m in range(8)]
            part, base = g // 8, 8 * (g % 8)
            for i in range(8):
                place = pl.ds(pl.multiple_of(part * 64 + group * 16, 16), 16)
                coeff_ref[base + i, place, lanes] = tiles[(-i) % 8]
        return carry

    lax.fori_loop(0, chunks * 4, step, 0)
    pl.semaphore_wait(barrier, devices - 1)
    left, sign, upper = packed_masks()

    def gram(f):
        block = coeff_ref[f]
        full = lax.dot_general(
            block, block, (((1,), (1,)), ((), ())), preferred_element_type=jnp.float32
        )
        packed = full[:64] + pltpu.roll(full[64:], 64, 1) * sign
        turned = pltpu.roll(packed, 64, 1)
        top = jnp.where(upper, packed, turned)
        bottom = jnp.where(upper, turned, packed)
        gram_ref[f] = jnp.where(left[:32], top[:32], bottom[32:])

    def give(f):
        owner = 2 * f + f % 2
        return pltpu.make_async_remote_copy(
            src_ref=gram_ref.at[f],
            dst_ref=slots.at[me],
            send_sem=sum_send,
            recv_sem=sum_recv,
            device_id=device(owner),
            device_id_type=MESH,
        )

    def gram_step(i, carry):
        gram((mine + 1 + i) % NF)

        @pl.when(i > 0)
        def _():
            give((mine + i) % NF).start()

        return carry

    lax.fori_loop(0, NF, gram_step, 0)
    pad = 48 + 2 * ((7 + mine) % 8) + 1

    def all_of(ref, count, sem):
        part = ref.at[pl.ds(0, count)]
        pltpu.make_async_copy(part, part, sem).wait()

    @pl.when(jnp.logical_not(is_owner))
    def _():
        give(mine).start()
        all_of(gram_ref, NF, sum_send)
        all_of(share_ref, NF, share_recv)

    @pl.when(is_owner)
    def _():
        slots[me] = gram_ref[mine]
        start = start_tile(start_ref, mine)
        all_of(slots, devices - 1, sum_recv)

        def add(i, total):
            for j in range(8):
                total = total + slots[i * 8 + j]
            return total

        packed = lax.fori_loop(0, devices // 8, add, jnp.zeros((32, 128), jnp.float32))
        share_ref[mine] = solve_tile(packed, start, pad, total_rows)
        all_of(gram_ref, NF - 1, sum_send)

        def share(k, carry):
            pltpu.make_async_remote_copy(
                src_ref=share_ref.at[mine],
                dst_ref=share_ref.at[mine],
                send_sem=share_send,
                recv_sem=share_recv,
                device_id=device((me + k) % devices),
                device_id_type=MESH,
            ).start()
            return carry

        lax.fori_loop(1, devices, share, 0)
        all_of(share_ref, NF - 1, share_recv)
        for count in (NF, devices - 1 - NF):
            all_of(share_ref, count, share_send)


def start_tile(start_ref, mine):
    lane = lax.broadcasted_iota(jnp.int32, (8, 128), 1)
    ours = lax.broadcasted_iota(jnp.int32, (8, NF), 1) == mine
    tile = jnp.zeros((8, 128), jnp.float32)

    def one(b, tile):
        word, e = b // 2, b % 2
        place = 16 * (word // 8) + 2 * ((word % 8 + mine) % 8) + e
        for p in range(2):
            column = jnp.sum(jnp.where(ours, start_ref[p, b], 0.0), axis=1, keepdims=True)
            tile = jnp.where(lane == 64 * p + place, column, tile)
        return tile

    return lax.fori_loop(0, NBLK, one, tile)


def transform(total_rows, devices, inner, snapshots, tables, weights, field, start):
    rows, lanes = snapshots.shape
    vmem = pl.BlockSpec(memory_space=pltpu.VMEM)
    return pl.pallas_call(
        functools.partial(transform_kernel, total_rows, devices, inner),
        out_shape=(
            pltpu.VMEM((NF, 128, lanes), jnp.bfloat16),
            pltpu.VMEM((NF, 16, 128), jnp.float32),
        ),
        in_specs=[pl.BlockSpec(memory_space=pltpu.HBM), vmem, vmem, vmem, vmem],
        out_specs=(vmem, vmem),
        scratch_shapes=[
            pltpu.VMEM((2, rows + 128, XC), jnp.bfloat16),
            pltpu.VMEM((8, 256, XC), jnp.bfloat16),
            pltpu.VMEM((NF, 32, 128), jnp.float32),
            pltpu.VMEM((devices, 32, 128), jnp.float32),
            pltpu.SemaphoreType.DMA((2, 4)),
            pltpu.SemaphoreType.DMA,
            pltpu.SemaphoreType.DMA,
            pltpu.SemaphoreType.DMA,
            pltpu.SemaphoreType.DMA,
        ],
        compiler_params=pltpu.CompilerParams(
            vmem_limit_bytes=32 << 20, collective_id=0, has_side_effects=True
        ),
        name="transform",
    )(snapshots, tables, weights, field, start)


def split3(x):
    first = x.astype(jnp.bfloat16).astype(jnp.float32)
    rest = x - first
    second = rest.astype(jnp.bfloat16).astype(jnp.float32)
    return first, second, rest - second


def solve_tile(packed, start, pad, total_rows):
    row = lax.broadcasted_iota(jnp.int32, (64, 128), 0)
    lane = lax.broadcasted_iota(jnp.int32, (64, 128), 1)
    left = lane < 64
    stacked = jnp.concatenate([packed, pltpu.roll(packed, 64, 1)], axis=0)
    stacked = jnp.where(left, stacked, 0.0)
    square = jnp.concatenate([stacked, jnp.zeros_like(stacked)], axis=0)
    flipped = jnp.transpose(square)[:64]
    real = jnp.where(row <= lane, stacked, flipped)
    imag = jnp.where(row > lane, stacked, jnp.where(row < lane, -flipped, 0.0))
    real = jnp.where(left, real, 0.0)
    imag = jnp.where(left, imag, 0.0)
    at_pad = row == pad
    root_total = 1.0 / math.sqrt(total_rows)
    proj_real = jnp.sum(jnp.where(at_pad, real, 0.0), axis=0, keepdims=True) * root_total
    proj_imag = jnp.sum(jnp.where(at_pad, imag, 0.0), axis=0, keepdims=True) * root_total
    inside = jnp.logical_and(jnp.logical_not(at_pad), lane != pad)
    inside_line = lax.broadcasted_iota(jnp.int32, (1, 128), 1) != pad
    proj_real = jnp.where(inside_line, proj_real, 0.0)
    proj_imag = jnp.where(inside_line, proj_imag, 0.0)
    real = jnp.where(inside, real, 0.0) * (1.0 / total_rows)
    imag = jnp.where(inside, imag, 0.0) * (1.0 / total_rows)
    weight = jnp.concatenate(
        [real - pltpu.roll(imag, 64, 1), imag + pltpu.roll(real, 64, 1)], axis=0
    )
    w1, w2, w3 = split3(weight)
    wide = jnp.concatenate([w1, w2, w3], axis=1).astype(jnp.bfloat16)
    left8 = lax.broadcasted_iota(jnp.int32, (8, 128), 1) < 64
    sign8 = jnp.where(left8, 1.0, -1.0)
    row8 = lax.broadcasted_iota(jnp.int32, (8, 128), 0)

    def image(v):
        v1, v2, v3 = split3(v)
        stack = jnp.concatenate([v1, v2, v3, jnp.zeros_like(v3)], axis=0).astype(jnp.bfloat16)
        out = jnp.dot(stack, wide, preferred_element_type=jnp.float32)
        small = out[:8, 256:] + out[8:16, 128:256] + out[16:24, :128]
        return (small + (out[:8, 128:256] + out[8:16, :128])) + out[:8, :128]

    def total(x):
        return jnp.sum(x, axis=1, keepdims=True)

    def sweep(index, v):
        y = image(v)
        x = pltpu.roll(y, 64, 1) * sign8
        norms = jnp.zeros((8, 128), jnp.float32)
        for j in range(NM):
            yj = jnp.broadcast_to(y[j : j + 1], (8, 128))
            c_real = jnp.broadcast_to(total(yj * y), (8, 128))
            norm = jnp.broadcast_to(c_real[j : j + 1], (8, 128)) + 1e-06
            norms = jnp.where(row8 == j, norm, norms)
            if j + 1 < NM:
                xj = jnp.broadcast_to(x[j : j + 1], (8, 128))
                c_imag = jnp.broadcast_to(total(yj * x), (8, 128))
                scale = jnp.where(row8 > j, 1.0 / norm, 0.0)
                a, b = c_real * scale, c_imag * scale
                y, x = y - (a * yj - b * xj), x - (a * xj + b * yj)
        return y / jnp.sqrt(norms)

    basis = lax.fori_loop(0, ITERS, sweep, start)
    energy = total(basis * image(basis))
    coef = basis.astype(jnp.bfloat16).astype(jnp.float32)
    proj_one = proj_real - pltpu.roll(proj_imag, 64, 1)
    proj_two = proj_imag + pltpu.roll(proj_real, 64, 1)
    corr_real = total(coef * proj_one)
    corr_imag = total(coef * proj_two)
    gain = 1.0 / jnp.sqrt(energy + 1e-06)
    tilt_real = gain * corr_real
    tilt_imag = gain * corr_imag
    size = jnp.sqrt(jnp.maximum(tilt_real * tilt_real + tilt_imag * tilt_imag, 0.25))
    factor_real = gain * tilt_real / size
    factor_imag = -gain * tilt_imag / size
    lane8 = lax.broadcasted_iota(jnp.int32, (8, 128), 1)
    facts = jnp.where(lane8 == 0, factor_real, jnp.where(lane8 == 1, factor_imag, energy))
    return jnp.concatenate([coef, facts], axis=0)


def project_kernel(coeff_ref, share_ref, weight_ref, out_ref, energy_ref):
    inverse = 1.0 / jnp.sqrt(weight_ref[...])
    lane = lax.broadcasted_iota(jnp.int32, (8, 128), 1)
    sign = jnp.where(lane < 64, 1.0, -1.0)
    place = lax.broadcasted_iota(jnp.int32, (8, NF), 1)
    step = out_ref.shape[0]
    first = pl.program_id(0) * step
    energies = energy_ref[...]
    for i in range(step):
        coef = share_ref[first + i, :8]
        rows16 = jnp.concatenate([coef * sign, pltpu.roll(coef, 64, 1)], axis=0)
        image = jnp.dot(
            rows16.astype(jnp.bfloat16), coeff_ref[first + i], preferred_element_type=jnp.float32
        )
        real, imag = image[:8], image[8:]
        turn_real, turn_imag = share_ref[first + i, 8:, 0:1], share_ref[first + i, 8:, 1:2]
        out_ref[i, :8] = (real * turn_real - imag * turn_imag) * inverse
        out_ref[i, 8:] = (real * turn_imag + imag * turn_real) * inverse
        energies = jnp.where(place == first + i, share_ref[first + i, 8:, 2:3], energies)
    energy_ref[...] = energies


def project(coeffs, shares, weights):
    lanes = coeffs.shape[2]
    step = 8
    vmem = pl.BlockSpec(memory_space=pltpu.VMEM)
    return pl.pallas_call(
        project_kernel,
        grid=(NF // step,),
        out_shape=(
            jax.ShapeDtypeStruct((NF, 2 * NM, lanes), jnp.float32),
            jax.ShapeDtypeStruct((NM, NF), jnp.float32),
        ),
        in_specs=[vmem, vmem, pl.BlockSpec((1, lanes), lambda i: (0, 0))],
        out_specs=(
            pl.BlockSpec((step, 16, lanes), lambda i: (i, 0, 0)),
            pl.BlockSpec((NM, NF), lambda i: (0, 0)),
        ),
        compiler_params=pltpu.CompilerParams(vmem_limit_bytes=6 << 20),
        name="project",
    )(coeffs, shares, weights)


def shards(snapshots, weights, reference_field, start_basis):
    axes = ("grp", "row")
    devices, inner = lax.axis_size(axes), lax.axis_size("row")
    total_rows = snapshots.shape[1] * devices
    start = jnp.transpose(start_basis, (1, 2, 3, 0))
    coeffs, shares = transform(
        total_rows, devices, inner,
        snapshots, jnp.asarray(pair_tables()), weights[None], reference_field[None], start,
    )
    modes, energies = project(coeffs, shares, weights[None])
    return modes, energies.T


def solution(mesh):
    in_specs = (P(None, ("grp", "row")), P(("grp", "row")), P(("grp", "row")), P())
    out_specs = (P(None, None, ("grp", "row")), P())
    return jax.shard_map(shards, mesh=mesh, in_specs=in_specs, out_specs=out_specs, check_vma=False)
```

profile of v0, /device:TPU:1, one launch (start us, length us, event | category | flops | bytes accessed | tf_op | source)
XLA Modules:
  0.0 81.4 jit_solution(12051921781597858752)
XLA Ops:
  0.6 0.0 copy-start
  0.6 1.4 %copy-done = bf16[8,256,384]{2,1,0:T(8,128)(2,1)S(1)} copy-done((bf16[8,256,384]{2,1,0:T(8,128)(2,1)S(1)}, bf16[8,256,384]{2,1,0:T(8,128)(2,1)}, u32[]{:S(2)}) %copy-start) | copy-done | bytes 1572888
  2.0 0.0 copy-start.1
  2.0 1.0 %copy-done.1 = f32[64,2,63,8]{0,3,2,1:T(8,128)S(1)} copy-done((f32[64,2,63,8]{0,3,2,1:T(8,128)S(1)}, f32[64,2,63,8]{0,3,2,1:T(8,128)}, u32[]{:S(2)}) %copy-start.1) | copy-done | bytes 258072
  3.1 0.0 copy-start.2
  3.1 0.7 copy-done.2
  3.8 0.0 copy-start.3
  3.8 0.7 copy-done.3
  4.5 71.5 %transform.1 = (bf16[64,128,1024]{2,1,0:T(8,128)(2,1)S(1)}, f32[64,16,128]{2,1,0:T(8,128)S(1)}) custom-call(bf16[8192,1024]{1,0:T(8,128)(2,1)} %snap_ref.1, bf16[8,256,384]{2,1,0:T(8,128)(2,1)S(1)} %copy-done, f32[1,1024]{1,0:T(1,128)S(1)} %bitcast.5, f32[1,1024]{1,0:T(1,128)S(1)} %bitcast.7, f32[2,63,8,64]{3,2,1,0:T(8,128)S(1)} %bitcast.4), custom_call_target="tpu_custom_call" | custom-call | tf_op jit(solution)/shard_map/transform/pallas_call | solution.py:238
  75.9 5.4 %project.1 = (f32[64,16,1024]{2,1,0:T(8,128)}, f32[8,64]{1,0:T(8,128)}) custom-call(bf16[64,128,1024]{2,1,0:T(8,128)(2,1)S(1)} %get-tuple-element.6.coeff_ref, f32[64,16,128]{2,1,0:T(8,128)S(1)} %get-tuple-element.7.share_ref, f32[1,1024]{1,0:T(1,128)S(1)} %bitcast.6), custom_call_target="tpu_custom_call" | custom-call | tf_op jit(solution)/shard_map/project/pallas_call | solution.py:373
Async XLA Ops:
  0.6 1.4 %copy-start = (bf16[8,256,384]{2,1,0:T(8,128)(2,1)S(1)}, bf16[8,256,384]{2,1,0:T(8,128)(2,1)}, u32[]{:S(2)}) copy-start(bf16[8,256,384]{2,1,0:T(8,128)(2,1)} %constant.2.clone.table_ref) | copy-start | bytes 4718596
  2.0 1.0 %copy-start.1 = (f32[64,2,63,8]{0,3,2,1:T(8,128)S(1)}, f32[64,2,63,8]{0,3,2,1:T(8,128)}, u32[]{:S(2)}) copy-start(f32[64,2,63,8]{0,3,2,1:T(8,128)} %param.8) | copy-start | bytes 774148
  3.1 0.7 copy-start.2
  3.8 0.7 copy-start.3
where the time goes:
time: 81.6 us; the launch traced here: 81.4 us
  Pallas kernels  76.9 us (94%)
  local copies, waits for them, and re-layouts  3.81 us (5%)
    pallas_call x1, Pallas kernels, transform(): pl.pallas_call(functools.partial(transform_kernel, total_rows, devices, i...  71.5 us
    pallas_call x1, Pallas kernels, project(): pl.pallas_call(project_kernel, grid=(NF // step,), out_shape=(jax.ShapeDt...  5.42 us
    unnamed x8, local copies, waits for them, and re-layouts  3.81 us

commit v1 on v0

--- a/solution.py
+++ b/solution.py
@@ -15,6 +15,7 @@
 NM = 8
 ITERS = 12
 XC = 256
+GRAMS = 4
 MESH = pl.DeviceIdType.MESH
 
 
@@ -52,27 +53,30 @@
 
 def transform_kernel(
     total_rows, devices, inner,
-    snap_ref, table_ref, weight_ref, field_ref, start_ref,
+    snap_ref, table_hbm, weight_hbm, field_hbm, start_hbm,
     coeff_ref, share_ref,
-    buf, stage, gram_ref, slots, snap_sems, sum_send, sum_recv, share_send, share_recv,
+    buf, stage_a, stage_b, table_ref, weight_ref, field_ref, start_ref, gram_ref, pair_slots, slots,
+    snap_sems, side_sems, pair_sems, sum_send, sum_recv, share_send, share_recv,
 ):
     pieces = 4
     piece_rows = snap_ref.shape[0] // pieces
     chunks = snap_ref.shape[1] // XC
     rows = snap_ref.shape[0]
+    chips = devices // 2
     grp, row = lax.axis_index("grp"), lax.axis_index("row")
     me = grp * inner + row
-    mine = me // 2
-    is_owner = row % 2 == mine % 2
+    mine = lax.div(me, 2)
+    core = lax.rem(me, 2)
+    is_owner = core == lax.rem(mine, 2)
 
     def device(index):
-        return (index // inner, index % inner)
+        return (lax.div(index, inner), lax.rem(index, inner))
 
     barrier = pltpu.get_barrier_semaphore()
 
-    def greet(k, carry):
-        pl.semaphore_signal(barrier, inc=1, device_id=device((me + k) % devices), device_id_type=MESH)
-        return carry
+    def greet(k):
+        there = lax.rem(me + k, devices)
+        pl.semaphore_signal(barrier, inc=1, device_id=device(there), device_id_type=MESH)
 
     def piece_copy(chunk, slot, piece):
         lanes = pl.ds(pl.multiple_of(chunk * XC, XC), XC)
@@ -81,63 +85,73 @@
             snap_ref.at[span, lanes], buf.at[slot, span, :], snap_sems.at[slot, piece]
         )
 
+    side = [
+        pltpu.make_async_copy(source, target, side_sems.at[i])
+        for i, (source, target) in enumerate((
+            (weight_hbm, weight_ref), (field_hbm, field_ref), (table_hbm, table_ref), (start_hbm, start_ref),
+        ))
+    ]
+    side[2].start()
     for piece in range(pieces):
         piece_copy(0, 0, piece).start()
-    lax.fori_loop(1, devices, greet, 0)
+    for i in (0, 1, 3):
+        side[i].start()
     for slot in range(2):
         buf[slot, rows:, :] = jnp.zeros((128, XC), jnp.bfloat16)
     word = lax.broadcasted_iota(jnp.int32, (16, XC), 0) // 2
-    odd_row = lax.broadcasted_iota(jnp.int32, (256, XC), 0)
-    is_odd = odd_row % 2 == 1
-    real_half = odd_row < 128
+    row256 = lax.broadcasted_iota(jnp.int32, (256, XC), 0)
+    is_odd = row256 % 2 == 1
+    real_half = row256 < 128
     bits = [(word // s) % 2 == 1 for s in (1, 2, 4)]
-
-    def step(s, carry):
-        chunk, group = s // 4, s % 4
-        slot = chunk % 2
+    stages = (stage_a, stage_b)
+    for i in range(4):
+        side[i].wait()
+
+    def network(source, g, group, lanes):
+        tiles = [source[r, 16 * g : 16 * g + 16, :] for r in range(8)]
+        for level, bit in zip((1, 2, 4), bits):
+            tiles = [jnp.where(bit, tiles[(m + level) % 8], tiles[m]) for m in range(8)]
+        part, base = g // 8, 8 * (g % 8)
+        for i in range(8):
+            first = part * 64 + group * 16
+            coeff_ref[base + i, first : first + 16, lanes] = tiles[(-i) % 8]
+
+    def chunk_step(chunk, carry):
+        slot = lax.rem(chunk, 2)
         lanes = pl.ds(pl.multiple_of(chunk * XC, XC), XC)
-
-        @pl.when(jnp.logical_and(group == 0, chunk + 1 < chunks))
+        before = pl.ds(pl.multiple_of(lax.rem(chunk + chunks - 1, chunks) * XC, XC), XC)
+
+        @pl.when(chunk + 1 < chunks)
         def _():
             for piece in range(pieces):
                 piece_copy(chunk + 1, 1 - slot, piece).start()
 
-        @pl.when(group == 0)
-        def _():
-            piece_copy(chunk, slot, 0).wait()
-            piece_copy(chunk, slot, 1).wait()
-
-        @pl.when(group == 1)
-        def _():
-            piece_copy(chunk, slot, 2).wait()
-
-        @pl.when(group == 2)
-        def _():
-            piece_copy(chunk, slot, 3).wait()
-
         root = jnp.sqrt(weight_ref[:, lanes])
-        for r in range(8):
-            first = pl.multiple_of((group * 8 + r) * 256, 256)
-            out = jnp.dot(
-                table_ref[r], buf[slot, pl.ds(first, 384), :], preferred_element_type=jnp.float32
-            )
-            out = out * root
-            if r == 7:
-                probe = jnp.where(real_half, root * field_ref[:, lanes], 0.0)
-                out = jnp.where(jnp.logical_and(is_odd, group == 3), probe, out)
-            stage[r] = out.astype(jnp.bfloat16)
-        for g in range(16):
-            tiles = [stage[r, 16 * g : 16 * g + 16, :] for r in range(8)]
-            for level, bit in zip((1, 2, 4), bits):
-                tiles = [jnp.where(bit, tiles[(m + level) % 8], tiles[m]) for m in range(8)]
-            part, base = g // 8, 8 * (g % 8)
-            for i in range(8):
-                place = pl.ds(pl.multiple_of(part * 64 + group * 16, 16), 16)
-                coeff_ref[base + i, place, lanes] = tiles[(-i) % 8]
+        piece_copy(chunk, slot, 0).wait()
+        for group in range(4):
+            if group < 3:
+                piece_copy(chunk, slot, group + 1).wait()
+            target, source = stages[group % 2], stages[(group + 1) % 2]
+            for r in range(8):
+                first = (group * 8 + r) * 256
+                out = jnp.dot(
+                    table_ref[r], buf[slot, first : first + 384, :], preferred_element_type=jnp.float32
+                )
+                out = out * root
+                if r == 7 and group == 3:
+                    probe = jnp.where(real_half, root * field_ref[:, lanes], 0.0)
+                    out = jnp.where(is_odd, probe, out)
+                target[r] = out.astype(jnp.bfloat16)
+                for g in (2 * r, 2 * r + 1):
+                    network(source, g, (group + 3) % 4, before if group == 0 else lanes)
+            for k in range(8):
+                greet((chunk * 4 + group) * 8 + k + 1)
         return carry
 
-    lax.fori_loop(0, chunks * 4, step, 0)
-    pl.semaphore_wait(barrier, devices - 1)
+    lax.fori_loop(0, chunks, chunk_step, 0)
+    for g in range(16):
+        network(stages[1], g, 3, slice((chunks - 1) * XC, chunks * XC))
+    pl.semaphore_wait(barrier, chunks * 32)
     left, sign, upper = packed_masks()
 
     def gram(f):
@@ -149,30 +163,71 @@
         turned = pltpu.roll(packed, 64, 1)
         top = jnp.where(upper, packed, turned)
         bottom = jnp.where(upper, turned, packed)
-        gram_ref[f] = jnp.where(left[:32], top[:32], bottom[32:])
-
-    def give(f):
-        owner = 2 * f + f % 2
+        return jnp.where(left[:32], top[:32], bottom[32:])
+
+    def nth(q, parity):
+        return 2 * lax.rem(lax.div(mine, 2) + 1 + q, NF // 2) + parity
+
+    def pair_give(f):
         return pltpu.make_async_remote_copy(
             src_ref=gram_ref.at[f],
-            dst_ref=slots.at[me],
+            dst_ref=pair_slots.at[lax.div(f, 2)],
+            send_sem=sum_send,
+            recv_sem=pair_sems.at[lax.div(f, 2)],
+            device_id=device(me + 1 - 2 * core),
+            device_id_type=MESH,
+        )
+
+    def give(f):
+        return pltpu.make_async_remote_copy(
+            src_ref=gram_ref.at[f],
+            dst_ref=slots.at[mine],
             send_sem=sum_send,
             recv_sem=sum_recv,
-            device_id=device(owner),
+            device_id=device(2 * f + core),
             device_id_type=MESH,
         )
 
-    def gram_step(i, carry):
-        gram((mine + 1 + i) % NF)
+    def partner_step(i, carry):
+        for u in range(GRAMS):
+            f = nth(i * GRAMS + u, 1 - core)
+            gram_ref[f] = gram(f)
 
         @pl.when(i > 0)
         def _():
-            give((mine + i) % NF).start()
+            for u in range(GRAMS):
+                pair_give(nth((i - 1) * GRAMS + u, 1 - core)).start()
 
         return carry
 
-    lax.fori_loop(0, NF, gram_step, 0)
-    pad = 48 + 2 * ((7 + mine) % 8) + 1
+    trips = NF // 2 // GRAMS
+    lax.fori_loop(0, trips, partner_step, 0)
+
+    def own_step(i, carry):
+        for u in range(GRAMS):
+            f = nth(i * GRAMS + u, core)
+            half = lax.div(f, 2)
+            pltpu.make_async_copy(pair_slots.at[half], pair_slots.at[half], pair_sems.at[half]).wait()
+        for u in range(GRAMS):
+            f = nth(i * GRAMS + u, core)
+            gram_ref[f] = gram(f) + pair_slots[lax.div(f, 2)]
+
+        @pl.when(i == 0)
+        def _():
+            for u in range(GRAMS):
+                pair_give(nth((trips - 1) * GRAMS + u, 1 - core)).start()
+
+        @pl.when(i > 0)
+        def _():
+            for u in range(GRAMS):
+                give(nth((i - 1) * GRAMS + u, core)).start()
+
+        return carry
+
+    lax.fori_loop(0, trips, own_step, 0)
+    for u in range(GRAMS - 1):
+        give(nth((trips - 1) * GRAMS + u, core)).start()
+    pad = 48 + 2 * lax.rem(7 + mine, 8) + 1
 
     def all_of(ref, count, sem):
         part = ref.at[pl.ds(0, count)]
@@ -180,22 +235,22 @@
 
     @pl.when(jnp.logical_not(is_owner))
     def _():
-        give(mine).start()
+        give(nth(NF // 2 - 1, core)).start()
         all_of(gram_ref, NF, sum_send)
         all_of(share_ref, NF, share_recv)
 
     @pl.when(is_owner)
     def _():
-        slots[me] = gram_ref[mine]
+        slots[mine] = gram_ref[mine]
         start = start_tile(start_ref, mine)
-        all_of(slots, devices - 1, sum_recv)
+        all_of(slots, chips - 1, sum_recv)
 
         def add(i, total):
             for j in range(8):
                 total = total + slots[i * 8 + j]
             return total
 
-        packed = lax.fori_loop(0, devices // 8, add, jnp.zeros((32, 128), jnp.float32))
+        packed = lax.fori_loop(0, chips // 8, add, jnp.zeros((32, 128), jnp.float32))
         share_ref[mine] = solve_tile(packed, start, pad, total_rows)
         all_of(gram_ref, NF - 1, sum_send)
 
@@ -205,7 +260,7 @@
                 dst_ref=share_ref.at[mine],
                 send_sem=share_send,
                 recv_sem=share_recv,
-                device_id=device((me + k) % devices),
+                device_id=device(lax.rem(me + k, devices)),
                 device_id_type=MESH,
             ).start()
             return carry
@@ -239,23 +294,31 @@
         functools.partial(transform_kernel, total_rows, devices, inner),
         out_shape=(
             pltpu.VMEM((NF, 128, lanes), jnp.bfloat16),
-            pltpu.VMEM((NF, 16, 128), jnp.float32),
+            pltpu.VMEM((NF, 16, 128), jnp.bfloat16),
         ),
-        in_specs=[pl.BlockSpec(memory_space=pltpu.HBM), vmem, vmem, vmem, vmem],
+        in_specs=[pl.BlockSpec(memory_space=pltpu.HBM)] * 5,
         out_specs=(vmem, vmem),
         scratch_shapes=[
             pltpu.VMEM((2, rows + 128, XC), jnp.bfloat16),
             pltpu.VMEM((8, 256, XC), jnp.bfloat16),
+            pltpu.VMEM((8, 256, XC), jnp.bfloat16),
+            pltpu.VMEM(tables.shape, tables.dtype),
+            pltpu.VMEM(weights.shape, weights.dtype),
+            pltpu.VMEM(field.shape, field.dtype),
+            pltpu.VMEM(start.shape, start.dtype),
             pltpu.VMEM((NF, 32, 128), jnp.float32),
-            pltpu.VMEM((devices, 32, 128), jnp.float32),
+            pltpu.VMEM((NF // 2, 32, 128), jnp.float32),
+            pltpu.VMEM((devices // 2, 32, 128), jnp.float32),
             pltpu.SemaphoreType.DMA((2, 4)),
+            pltpu.SemaphoreType.DMA((4,)),
+            pltpu.SemaphoreType.DMA((NF // 2,)),
             pltpu.SemaphoreType.DMA,
             pltpu.SemaphoreType.DMA,
             pltpu.SemaphoreType.DMA,
             pltpu.SemaphoreType.DMA,
         ],
         compiler_params=pltpu.CompilerParams(
-            vmem_limit_bytes=32 << 20, collective_id=0, has_side_effects=True
+            vmem_limit_bytes=48600 * 1024, collective_id=0, has_side_effects=True
         ),
         name="transform",
     )(snapshots, tables, weights, field, start)
@@ -309,24 +372,60 @@
     def total(x):
         return jnp.sum(x, axis=1, keepdims=True)
 
+    def scaled(y, norms):
+        inverse = lax.rsqrt(norms)
+        inverse = inverse * (1.5 - 0.5 * norms * inverse * inverse)
+        return y * inverse
+
+    def line(t, j):
+        return jnp.broadcast_to(t[j : j + 1], (8, 128))
+
+    def inner(t, u):
+        return jnp.broadcast_to(total(t * u), (8, 128))
+
+    def direct(v):
+        y = image(v)
+        x = pltpu.roll(y, 64, 1) * sign8
+        norms = jnp.zeros((8, 128), jnp.float32)
+        for j in range(NM):
+            yj = line(y, j)
+            c_real = inner(yj, y)
+            norm = line(c_real, j) + 1e-06
+            norms = jnp.where(row8 == j, norm, norms)
+            if j + 1 < NM:
+                xj = line(x, j)
+                c_imag = inner(yj, x)
+                scale = jnp.where(row8 > j, 1.0 / norm, 0.0)
+                a, b = c_real * scale, c_imag * scale
+                y, x = y - (a * yj - b * xj), x - (a * xj + b * yj)
+        return scaled(y, norms)
+
     def sweep(index, v):
         y = image(v)
         x = pltpu.roll(y, 64, 1) * sign8
         norms = jnp.zeros((8, 128), jnp.float32)
+        g_real = [inner(line(y, j), y) for j in range(NM)]
+        g_imag = [inner(line(y, j), x) for j in range(NM - 1)]
         for j in range(NM):
-            yj = jnp.broadcast_to(y[j : j + 1], (8, 128))
-            c_real = jnp.broadcast_to(total(yj * y), (8, 128))
-            norm = jnp.broadcast_to(c_real[j : j + 1], (8, 128)) + 1e-06
+            square_j = jnp.maximum(line(g_real[j], j), 0.0)
+            norm = square_j + 1e-06
             norms = jnp.where(row8 == j, norm, norms)
             if j + 1 < NM:
-                xj = jnp.broadcast_to(x[j : j + 1], (8, 128))
-                c_imag = jnp.broadcast_to(total(yj * x), (8, 128))
-                scale = jnp.where(row8 > j, 1.0 / norm, 0.0)
-                a, b = c_real * scale, c_imag * scale
+                yj, xj = line(y, j), line(x, j)
+                inverse = 1.0 / norm
+                scale = jnp.where(row8 > j, inverse, 0.0)
+                a, b = g_real[j] * scale, g_imag[j] * scale
                 y, x = y - (a * yj - b * xj), x - (a * xj + b * yj)
-        return y / jnp.sqrt(norms)
-
-    basis = lax.fori_loop(0, ITERS, sweep, start)
+                both = inverse * (2.0 - square_j * inverse)
+                e_real, e_imag = g_real[j] * both, g_imag[j] * both
+                for k in range(j + 1, NM):
+                    c_real, c_imag = line(g_real[j], k), line(g_imag[j], k)
+                    g_real[k] = g_real[k] - (c_real * e_real + c_imag * e_imag)
+                    if k + 1 < NM:
+                        g_imag[k] = g_imag[k] - (c_real * e_imag - c_imag * e_real)
+        return scaled(y, norms)
+
+    basis = direct(lax.fori_loop(1, ITERS - 1, sweep, direct(start)))
     energy = total(basis * image(basis))
     coef = basis.astype(jnp.bfloat16).astype(jnp.float32)
     proj_one = proj_real - pltpu.roll(proj_imag, 64, 1)
@@ -340,8 +439,11 @@
     factor_real = gain * tilt_real / size
     factor_imag = -gain * tilt_imag / size
     lane8 = lax.broadcasted_iota(jnp.int32, (8, 128), 1)
-    facts = jnp.where(lane8 == 0, factor_real, jnp.where(lane8 == 1, factor_imag, energy))
-    return jnp.concatenate([coef, facts], axis=0)
+    facts = jnp.zeros((8, 128), jnp.float32)
+    for i, value in enumerate((factor_real, factor_imag, energy)):
+        for j, piece in enumerate(split3(jnp.broadcast_to(value, (8, 128)))):
+            facts = jnp.where(lane8 == 3 * j + i, piece, facts)
+    return jnp.concatenate([coef, facts], axis=0).astype(jnp.bfloat16)
 
 
 def project_kernel(coeff_ref, share_ref, weight_ref, out_ref, energy_ref):
@@ -353,16 +455,18 @@
     first = pl.program_id(0) * step
     energies = energy_ref[...]
     for i in range(step):
-        coef = share_ref[first + i, :8]
+        tile = share_ref[first + i].astype(jnp.float32)
+        coef, parts = tile[:8], tile[8:]
+        facts = parts + pltpu.roll(parts, 125, 1) + pltpu.roll(parts, 122, 1)
         rows16 = jnp.concatenate([coef * sign, pltpu.roll(coef, 64, 1)], axis=0)
         image = jnp.dot(
             rows16.astype(jnp.bfloat16), coeff_ref[first + i], preferred_element_type=jnp.float32
         )
         real, imag = image[:8], image[8:]
-        turn_real, turn_imag = share_ref[first + i, 8:, 0:1], share_ref[first + i, 8:, 1:2]
+        turn_real, turn_imag = facts[:, 0:1], facts[:, 1:2]
         out_ref[i, :8] = (real * turn_real - imag * turn_imag) * inverse
         out_ref[i, 8:] = (real * turn_imag + imag * turn_real) * inverse
-        energies = jnp.where(place == first + i, share_ref[first + i, 8:, 2:3], energies)
+        energies = jnp.where(place == first + i, facts[:, 2:3], energies)
     energy_ref[...] = energies
 
 

time: 81.6 us -> 62.8 us (0.77)
  Pallas kernels: 76.9 us -> 62 us
  local copies, waits for them, and re-layouts: 3.81 us -> 0.01 us
    pallas_call x1, Pallas kernels: 71.5 us -> 56.6 us  [transform(): pl.pallas_call(functools.partial(transform_kernel, total_rows, devices, i...]
    unnamed x8 -> x2, local copies, waits for them, and re-layouts: 3.81 us -> 0.01 us
where the time goes in v1:
time: 62.8 us; the launch traced here: 62.7 us
  Pallas kernels  62 us (99%)
  between operations  0.65 us (1%)
    pallas_call x1, Pallas kernels, transform(): pl.pallas_call(functools.partial(transform_kernel, total_rows, devices, i...  56.6 us
    pallas_call x1, Pallas kernels, project(): pl.pallas_call(project_kernel, grid=(NF // step,), out_shape=(jax.ShapeDt...  5.43 us

profile of v1, /device:TPU:1, one launch (start us, length us, event | category | flops | bytes accessed | tf_op | source)
XLA Modules:
  0.0 62.7 jit_solution(3310014092477905407)
XLA Ops:
  0.6 0.0 copy-start
  0.6 56.6 %transform.1 = (bf16[64,128,1024]{2,1,0:T(8,128)(2,1)S(1)}, bf16[64,16,128]{2,1,0:T(8,128)(2,1)S(1)}) custom-call(bf16[8192,1024]{1,0:T(8,128)(2,1)} %snap_ref.1, bf16[8,256,384]{2,1,0:T(8,128)(2,1)} %constant.2.clone.table_hbm, f32[1,1024]{1,0:T(1,128)} %bitcast.4, f32[1,1024]{1,0:T(1,128)} %bitcast.7, f32[2,63,8,64]{3,2,1,0:T(8,128)} %bitcast.6), custom_call_target="tpu_custom_call" | custom-call | tf_op jit(solution)/shard_map/transform/pallas_call | solution.py:293
  57.2 0.0 copy-done
  57.2 5.4 %project.1 = (f32[64,16,1024]{2,1,0:T(8,128)}, f32[8,64]{1,0:T(8,128)}) custom-call(bf16[64,128,1024]{2,1,0:T(8,128)(2,1)S(1)} %get-tuple-element.6.coeff_ref, bf16[64,16,128]{2,1,0:T(8,128)(2,1)S(1)} %get-tuple-element.7.share_ref, f32[1,1024]{1,0:T(1,128)S(1)} %bitcast.5), custom_call_target="tpu_custom_call" | custom-call | tf_op jit(solution)/shard_map/project/pallas_call | solution.py:477
Async XLA Ops:
  0.6 56.6 %copy-start = (f32[1024]{0:T(1024)S(1)}, f32[1024]{0:T(1024)}, u32[]{:S(2)}) copy-start(f32[1024]{0:T(1024)} %param.6) | copy-start | bytes 12292

commit v2 on v1

--- a/solution.py
+++ b/solution.py
@@ -15,7 +15,6 @@
 NM = 8
 ITERS = 12
 XC = 256
-GRAMS = 4
 MESH = pl.DeviceIdType.MESH
 
 
@@ -55,7 +54,7 @@
     total_rows, devices, inner,
     snap_ref, table_hbm, weight_hbm, field_hbm, start_hbm,
     coeff_ref, share_ref,
-    buf, stage_a, stage_b, table_ref, weight_ref, field_ref, start_ref, gram_ref, pair_slots, slots,
+    buf, stage_a, stage_b, full_a, full_b, table_ref, weight_ref, field_ref, start_ref, gram_ref, pair_slots, slots,
     snap_sems, side_sems, pair_sems, sum_send, sum_recv, share_send, share_recv,
 ):
     pieces = 4
@@ -74,9 +73,18 @@
 
     barrier = pltpu.get_barrier_semaphore()
 
-    def greet(k):
-        there = lax.rem(me + k, devices)
-        pl.semaphore_signal(barrier, inc=1, device_id=device(there), device_id_type=MESH)
+    side_y = lax.rem(lax.div(row, 2), 4)
+    side_z = lax.div(row, 8)
+    xs = [lax.rem(grp + d, 4) for d in range(4)]
+    ys = [lax.rem(side_y + d, 4) for d in range(4)]
+    zs = [lax.rem(side_z + d, 4) for d in range(4)]
+    rows_of = {
+        (z, y, c): zs[z] * 8 + ys[y] * 2 + (1 - core if c else core)
+        for z in range(4) for y in range(4) for c in range(2)
+    }
+
+    def greet(there, key):
+        pl.semaphore_signal(barrier, inc=1, device_id=(there, rows_of[key]), device_id_type=MESH)
 
     def piece_copy(chunk, slot, piece):
         lanes = pl.ds(pl.multiple_of(chunk * XC, XC), XC)
@@ -127,10 +135,9 @@
                 piece_copy(chunk + 1, 1 - slot, piece).start()
 
         root = jnp.sqrt(weight_ref[:, lanes])
-        piece_copy(chunk, slot, 0).wait()
+        for piece in range(pieces):
+            piece_copy(chunk, slot, piece).wait()
         for group in range(4):
-            if group < 3:
-                piece_copy(chunk, slot, group + 1).wait()
             target, source = stages[group % 2], stages[(group + 1) % 2]
             for r in range(8):
                 first = (group * 8 + r) * 256
@@ -144,29 +151,40 @@
                 target[r] = out.astype(jnp.bfloat16)
                 for g in (2 * r, 2 * r + 1):
                     network(source, g, (group + 3) % 4, before if group == 0 else lanes)
-            for k in range(8):
-                greet((chunk * 4 + group) * 8 + k + 1)
+        there = lax.rem(grp + chunk, 4)
+        for key in rows_of:
+            if key != (0, 0, 0):
+                greet(there, key)
+
+        @pl.when(chunk > 0)
+        def _():
+            greet(there, (0, 0, 0))
+
         return carry
 
     lax.fori_loop(0, chunks, chunk_step, 0)
     for g in range(16):
         network(stages[1], g, 3, slice((chunks - 1) * XC, chunks * XC))
-    pl.semaphore_wait(barrier, chunks * 32)
+    pl.semaphore_wait(barrier, devices - 1)
     left, sign, upper = packed_masks()
+
+    def owner(parity, i, u):
+        far = (2, 3, 1, 0)
+        turn = lax.rem(parity + side_y, 2) + 2 * (1 - u % 2)
+        return xs[far[i]] * 16 + zs[far[u // 2]] * 4 + lax.rem(side_y + turn, 4)
 
     def gram(f):
         block = coeff_ref[f]
-        full = lax.dot_general(
+        return lax.dot_general(
             block, block, (((1,), (1,)), ((), ())), preferred_element_type=jnp.float32
         )
+
+    def pack(full):
         packed = full[:64] + pltpu.roll(full[64:], 64, 1) * sign
         turned = pltpu.roll(packed, 64, 1)
         top = jnp.where(upper, packed, turned)
         bottom = jnp.where(upper, turned, packed)
         return jnp.where(left[:32], top[:32], bottom[32:])
-
-    def nth(q, parity):
-        return 2 * lax.rem(lax.div(mine, 2) + 1 + q, NF // 2) + parity
 
     def pair_give(f):
         return pltpu.make_async_remote_copy(
@@ -188,45 +206,31 @@
             device_id_type=MESH,
         )
 
-    def partner_step(i, carry):
-        for u in range(GRAMS):
-            f = nth(i * GRAMS + u, 1 - core)
-            gram_ref[f] = gram(f)
-
-        @pl.when(i > 0)
-        def _():
-            for u in range(GRAMS):
-                pair_give(nth((i - 1) * GRAMS + u, 1 - core)).start()
-
-        return carry
-
-    trips = NF // 2 // GRAMS
-    lax.fori_loop(0, trips, partner_step, 0)
-
-    def own_step(i, carry):
-        for u in range(GRAMS):
-            f = nth(i * GRAMS + u, core)
-            half = lax.div(f, 2)
-            pltpu.make_async_copy(pair_slots.at[half], pair_slots.at[half], pair_sems.at[half]).wait()
-        for u in range(GRAMS):
-            f = nth(i * GRAMS + u, core)
-            gram_ref[f] = gram(f) + pair_slots[lax.div(f, 2)]
-
-        @pl.when(i == 0)
-        def _():
-            for u in range(GRAMS):
-                pair_give(nth((trips - 1) * GRAMS + u, 1 - core)).start()
-
-        @pl.when(i > 0)
-        def _():
-            for u in range(GRAMS):
-                give(nth((i - 1) * GRAMS + u, core)).start()
-
-        return carry
-
-    lax.fori_loop(0, trips, own_step, 0)
-    for u in range(GRAMS - 1):
-        give(nth((trips - 1) * GRAMS + u, core)).start()
+    order = ((0, 0), (0, 1), (1, 0), (0, 2), (1, 1), (0, 3), (1, 2), (1, 3))
+    batches = [
+        (own, [owner(core if own else 1 - core, i, u) for u in range(8)]) for own, i in order
+    ]
+    fulls = (full_a, full_b)
+    last = len(batches) - 1
+    for t in range(len(batches) + 1):
+        if t > 0 and batches[t - 1][0]:
+            for f in batches[t - 1][1]:
+                half = pair_slots.at[lax.div(f, 2)]
+                pltpu.make_async_copy(half, half, pair_sems.at[lax.div(f, 2)]).wait()
+        if t > 1:
+            for f in batches[t - 2][1]:
+                (give if batches[t - 2][0] else pair_give)(f).start()
+        for u in range(8):
+            if t <= last:
+                fulls[t % 2][u] = gram(batches[t][1][u])
+            if t > 0:
+                own, fs = batches[t - 1]
+                packed = pack(fulls[(t - 1) % 2][u])
+                if own:
+                    packed = packed + pair_slots[lax.div(fs[u], 2)]
+                gram_ref[fs[u]] = packed
+    for f in batches[last][1][:-1]:
+        give(f).start()
     pad = 48 + 2 * lax.rem(7 + mine, 8) + 1
 
     def all_of(ref, count, sem):
@@ -235,7 +239,7 @@
 
     @pl.when(jnp.logical_not(is_owner))
     def _():
-        give(nth(NF // 2 - 1, core)).start()
+        give(batches[last][1][-1]).start()
         all_of(gram_ref, NF, sum_send)
         all_of(share_ref, NF, share_recv)
 
@@ -254,18 +258,20 @@
         share_ref[mine] = solve_tile(packed, start, pad, total_rows)
         all_of(gram_ref, NF - 1, sum_send)
 
-        def share(k, carry):
+        def near(d):
+            return min(d, 4 - d)
+
+        peers = [(x, key) for x in range(4) for key in rows_of if (x, key) != (0, (0, 0, 0))]
+        peers.sort(key=lambda p: -(near(p[0]) + near(p[1][0]) + near(p[1][1])))
+        for x, key in peers:
             pltpu.make_async_remote_copy(
                 src_ref=share_ref.at[mine],
                 dst_ref=share_ref.at[mine],
                 send_sem=share_send,
                 recv_sem=share_recv,
-                device_id=device(lax.rem(me + k, devices)),
+                device_id=(xs[x], rows_of[key]),
                 device_id_type=MESH,
             ).start()
-            return carry
-
-        lax.fori_loop(1, devices, share, 0)
         all_of(share_ref, NF - 1, share_recv)
         for count in (NF, devices - 1 - NF):
             all_of(share_ref, count, share_send)
@@ -276,15 +282,17 @@
     ours = lax.broadcasted_iota(jnp.int32, (8, NF), 1) == mine
     tile = jnp.zeros((8, 128), jnp.float32)
 
-    def one(b, tile):
-        word, e = b // 2, b % 2
-        place = 16 * (word // 8) + 2 * ((word % 8 + mine) % 8) + e
-        for p in range(2):
-            column = jnp.sum(jnp.where(ours, start_ref[p, b], 0.0), axis=1, keepdims=True)
-            tile = jnp.where(lane == 64 * p + place, column, tile)
+    def some(i, tile):
+        for j in range(21):
+            b = i * 21 + j
+            word, e = lax.div(b, 2), lax.rem(b, 2)
+            place = 16 * lax.div(word, 8) + 2 * lax.rem(lax.rem(word, 8) + mine, 8) + e
+            for p in range(2):
+                column = jnp.sum(jnp.where(ours, start_ref[p, b], 0.0), axis=1, keepdims=True)
+                tile = jnp.where(lane == 64 * p + place, column, tile)
         return tile
 
-    return lax.fori_loop(0, NBLK, one, tile)
+    return lax.fori_loop(0, NBLK // 21, some, tile)
 
 
 def transform(total_rows, devices, inner, snapshots, tables, weights, field, start):
@@ -302,6 +310,8 @@
             pltpu.VMEM((2, rows + 128, XC), jnp.bfloat16),
             pltpu.VMEM((8, 256, XC), jnp.bfloat16),
             pltpu.VMEM((8, 256, XC), jnp.bfloat16),
+            pltpu.VMEM((8, 128, 128), jnp.float32),
+            pltpu.VMEM((8, 128, 128), jnp.float32),
             pltpu.VMEM(tables.shape, tables.dtype),
             pltpu.VMEM(weights.shape, weights.dtype),
             pltpu.VMEM(field.shape, field.dtype),

time: 62.8 us -> 57.8 us (0.920)
  Pallas kernels: 62 us -> 57 us
    pallas_call x1, Pallas kernels: 56.6 us -> 51.6 us  [transform(): pl.pallas_call(functools.partial(transform_kernel, total_rows, devices, i...]
where the time goes in v2:
time: 57.8 us; the launch traced here: 57.7 us
  Pallas kernels  57 us (99%)
  between operations  0.65 us (1%)
    pallas_call x1, Pallas kernels, transform(): pl.pallas_call(functools.partial(transform_kernel, total_rows, devices, i...  51.6 us
    pallas_call x1, Pallas kernels, project(): pl.pallas_call(project_kernel, grid=(NF // step,), out_shape=(jax.ShapeDt...  5.43 us

profile of v2, /device:TPU:1, one launch (start us, length us, event | category | flops | bytes accessed | tf_op | source)
XLA Modules:
  0.0 57.7 jit_solution(5124063714865971494)
XLA Ops:
  0.6 0.0 copy-start
  0.6 51.6 %transform.1 = (bf16[64,128,1024]{2,1,0:T(8,128)(2,1)S(1)}, bf16[64,16,128]{2,1,0:T(8,128)(2,1)S(1)}) custom-call(bf16[8192,1024]{1,0:T(8,128)(2,1)} %snap_ref.1, bf16[8,256,384]{2,1,0:T(8,128)(2,1)} %constant.2.clone.table_hbm, f32[1,1024]{1,0:T(1,128)} %bitcast.4, f32[1,1024]{1,0:T(1,128)} %bitcast.7, f32[2,63,8,64]{3,2,1,0:T(8,128)} %bitcast.6), custom_call_target="tpu_custom_call" | custom-call | tf_op jit(solution)/shard_map/transform/pallas_call | solution.py:301
  52.2 0.0 copy-done
  52.2 5.4 %project.1 = (f32[64,16,1024]{2,1,0:T(8,128)}, f32[8,64]{1,0:T(8,128)}) custom-call(bf16[64,128,1024]{2,1,0:T(8,128)(2,1)S(1)} %get-tuple-element.6.coeff_ref, bf16[64,16,128]{2,1,0:T(8,128)(2,1)S(1)} %get-tuple-element.7.share_ref, f32[1,1024]{1,0:T(1,128)S(1)} %bitcast.5), custom_call_target="tpu_custom_call" | custom-call | tf_op jit(solution)/shard_map/project/pallas_call | solution.py:487
Async XLA Ops:
  0.6 51.6 %copy-start = (f32[1024]{0:T(1024)S(1)}, f32[1024]{0:T(1024)}, u32[]{:S(2)}) copy-start(f32[1024]{0:T(1024)} %param.6) | copy-start | bytes 12292

commit v3 on v2

--- a/solution.py
+++ b/solution.py
@@ -53,8 +53,8 @@
 def transform_kernel(
     total_rows, devices, inner,
     snap_ref, table_hbm, weight_hbm, field_hbm, start_hbm,
-    coeff_ref, share_ref,
-    buf, stage_a, stage_b, full_a, full_b, table_ref, weight_ref, field_ref, start_ref, gram_ref, pair_slots, slots,
+    modes_ref, energy_ref,
+    coeff_ref, share_ref, buf, stage_a, stage_b, full_a, full_b, table_ref, weight_ref, field_ref, start_ref, gram_ref, pair_slots, slots,
     snap_sems, side_sems, pair_sems, sum_send, sum_recv, share_send, share_recv,
 ):
     pieces = 4
@@ -99,11 +99,11 @@
             (weight_hbm, weight_ref), (field_hbm, field_ref), (table_hbm, table_ref), (start_hbm, start_ref),
         ))
     ]
-    side[2].start()
+    for i in (0, 1, 2):
+        side[i].start()
     for piece in range(pieces):
         piece_copy(0, 0, piece).start()
-    for i in (0, 1, 3):
-        side[i].start()
+    side[3].start()
     for slot in range(2):
         buf[slot, rows:, :] = jnp.zeros((128, XC), jnp.bfloat16)
     word = lax.broadcasted_iota(jnp.int32, (16, XC), 0) // 2
@@ -112,7 +112,7 @@
     real_half = row256 < 128
     bits = [(word // s) % 2 == 1 for s in (1, 2, 4)]
     stages = (stage_a, stage_b)
-    for i in range(4):
+    for i in (0, 1, 2):
         side[i].wait()
 
     def network(source, g, group, lanes):
@@ -125,19 +125,29 @@
             coeff_ref[base + i, first : first + 16, lanes] = tiles[(-i) % 8]
 
     def chunk_step(chunk, carry):
-        slot = lax.rem(chunk, 2)
-        lanes = pl.ds(pl.multiple_of(chunk * XC, XC), XC)
-        before = pl.ds(pl.multiple_of(lax.rem(chunk + chunks - 1, chunks) * XC, XC), XC)
-
-        @pl.when(chunk + 1 < chunks)
-        def _():
+        first_chunk = isinstance(chunk, int)
+        if first_chunk:
+            slot, lanes, before = 0, slice(0, XC), None
             for piece in range(pieces):
-                piece_copy(chunk + 1, 1 - slot, piece).start()
+                piece_copy(1, 1, piece).start()
+            piece_copy(0, 0, 0).wait()
+        else:
+            slot = lax.rem(chunk, 2)
+            lanes = pl.ds(pl.multiple_of(chunk * XC, XC), XC)
+            before = pl.ds(pl.multiple_of((chunk - 1) * XC, XC), XC)
+
+            @pl.when(chunk + 1 < chunks)
+            def _():
+                for piece in range(pieces):
+                    piece_copy(chunk + 1, 1 - slot, piece).start()
+
+            for piece in range(pieces):
+                piece_copy(chunk, slot, piece).wait()
 
         root = jnp.sqrt(weight_ref[:, lanes])
-        for piece in range(pieces):
-            piece_copy(chunk, slot, piece).wait()
         for group in range(4):
+            if first_chunk and group < 3:
+                piece_copy(0, 0, group + 1).wait()
             target, source = stages[group % 2], stages[(group + 1) % 2]
             for r in range(8):
                 first = (group * 8 + r) * 256
@@ -149,20 +159,16 @@
                     probe = jnp.where(real_half, root * field_ref[:, lanes], 0.0)
                     out = jnp.where(is_odd, probe, out)
                 target[r] = out.astype(jnp.bfloat16)
-                for g in (2 * r, 2 * r + 1):
+                for g in (2 * r, 2 * r + 1) if group or not first_chunk else ():
                     network(source, g, (group + 3) % 4, before if group == 0 else lanes)
-        there = lax.rem(grp + chunk, 4)
+        there = grp if first_chunk else lax.rem(grp + chunk, 4)
         for key in rows_of:
-            if key != (0, 0, 0):
+            if not (first_chunk and key == (0, 0, 0)):
                 greet(there, key)
-
-        @pl.when(chunk > 0)
-        def _():
-            greet(there, (0, 0, 0))
-
         return carry
 
-    lax.fori_loop(0, chunks, chunk_step, 0)
+    chunk_step(0, 0)
+    lax.fori_loop(1, chunks, chunk_step, 0)
     for g in range(16):
         network(stages[1], g, 3, slice((chunks - 1) * XC, chunks * XC))
     pl.semaphore_wait(barrier, devices - 1)
@@ -237,15 +243,27 @@
         part = ref.at[pl.ds(0, count)]
         pltpu.make_async_copy(part, part, sem).wait()
 
+    def tile_came(f):
+        tile = share_ref.at[f]
+        pltpu.make_async_copy(tile, tile, share_recv.at[f]).wait()
+
+    def near(d):
+        return min(d, 4 - d)
+
+    def far_off(x, z, y):
+        return near(x) + near(z) + near(y)
+
     @pl.when(jnp.logical_not(is_owner))
     def _():
         give(batches[last][1][-1]).start()
         all_of(gram_ref, NF, sum_send)
-        all_of(share_ref, NF, share_recv)
+        side[3].wait()
+        tile_came(mine)
 
     @pl.when(is_owner)
     def _():
         slots[mine] = gram_ref[mine]
+        side[3].wait()
         start = start_tile(start_ref, mine)
         all_of(slots, chips - 1, sum_recv)
 
@@ -258,21 +276,47 @@
         share_ref[mine] = solve_tile(packed, start, pad, total_rows)
         all_of(gram_ref, NF - 1, sum_send)
 
-        def near(d):
-            return min(d, 4 - d)
-
         peers = [(x, key) for x in range(4) for key in rows_of if (x, key) != (0, (0, 0, 0))]
-        peers.sort(key=lambda p: -(near(p[0]) + near(p[1][0]) + near(p[1][1])))
+        peers.sort(key=lambda p: -far_off(p[0], *p[1][:2]))
         for x, key in peers:
             pltpu.make_async_remote_copy(
                 src_ref=share_ref.at[mine],
                 dst_ref=share_ref.at[mine],
                 send_sem=share_send,
-                recv_sem=share_recv,
+                recv_sem=share_recv.at[mine],
                 device_id=(xs[x], rows_of[key]),
                 device_id_type=MESH,
             ).start()
-        all_of(share_ref, NF - 1, share_recv)
+
+    inverse_root = 1.0 / jnp.sqrt(weight_ref[...])
+    lane8 = lax.broadcasted_iota(jnp.int32, (8, 128), 1)
+    sign8 = jnp.where(lane8 < 64, 1.0, -1.0)
+    place = lax.broadcasted_iota(jnp.int32, (NM, NF), 1)
+    steps = [(x, z, y) for x in range(4) for z in range(4) for y in range(4)]
+    steps.sort(key=lambda p: far_off(*p))
+    energies = jnp.zeros((NM, NF), jnp.float32)
+    bounds = (0, 22, 42, 57, 64)
+    for low, high in zip(bounds[:-1], bounds[1:]):
+        fs = [xs[x] * 16 + zs[z] * 4 + ys[y] for x, z, y in steps[low:high]]
+        for f in fs[1:] if low == 0 else fs:
+            tile_came(f)
+        for f in fs:
+            tile = share_ref[f].astype(jnp.float32)
+            coef, parts = tile[:8], tile[8:]
+            facts = parts + pltpu.roll(parts, 125, 1) + pltpu.roll(parts, 122, 1)
+            rows16 = jnp.concatenate([coef * sign8, pltpu.roll(coef, 64, 1)], axis=0)
+            image = jnp.dot(
+                rows16.astype(jnp.bfloat16), coeff_ref[f], preferred_element_type=jnp.float32
+            )
+            real, imag = image[:8], image[8:]
+            turn_real, turn_imag = facts[:, 0:1], facts[:, 1:2]
+            modes_ref[f, :8] = (real * turn_real - imag * turn_imag) * inverse_root
+            modes_ref[f, 8:] = (real * turn_imag + imag * turn_real) * inverse_root
+            energies = jnp.where(place == f, facts[:, 2:3], energies)
+    energy_ref[...] = energies
+
+    @pl.when(is_owner)
+    def _():
         for count in (NF, devices - 1 - NF):
             all_of(share_ref, count, share_send)
 
@@ -301,12 +345,14 @@
     return pl.pallas_call(
         functools.partial(transform_kernel, total_rows, devices, inner),
         out_shape=(
-            pltpu.VMEM((NF, 128, lanes), jnp.bfloat16),
-            pltpu.VMEM((NF, 16, 128), jnp.bfloat16),
+            pltpu.VMEM((NF, 2 * NM, lanes), jnp.float32),
+            pltpu.VMEM((NM, NF), jnp.float32),
         ),
         in_specs=[pl.BlockSpec(memory_space=pltpu.HBM)] * 5,
         out_specs=(vmem, vmem),
         scratch_shapes=[
+            pltpu.VMEM((NF, 128, lanes), jnp.bfloat16),
+            pltpu.VMEM((NF, 16, 128), jnp.bfloat16),
             pltpu.VMEM((2, rows + 128, XC), jnp.bfloat16),
             pltpu.VMEM((8, 256, XC), jnp.bfloat16),
             pltpu.VMEM((8, 256, XC), jnp.bfloat16),
@@ -325,10 +371,10 @@
             pltpu.SemaphoreType.DMA,
             pltpu.SemaphoreType.DMA,
             pltpu.SemaphoreType.DMA,
-            pltpu.SemaphoreType.DMA,
+            pltpu.SemaphoreType.DMA((NF,)),
         ],
         compiler_params=pltpu.CompilerParams(
-            vmem_limit_bytes=48600 * 1024, collective_id=0, has_side_effects=True
+            vmem_limit_bytes=61200 * 1024, collective_id=0, has_side_effects=True
         ),
         name="transform",
     )(snapshots, tables, weights, field, start)
@@ -456,61 +502,15 @@
     return jnp.concatenate([coef, facts], axis=0).astype(jnp.bfloat16)
 
 
-def project_kernel(coeff_ref, share_ref, weight_ref, out_ref, energy_ref):
-    inverse = 1.0 / jnp.sqrt(weight_ref[...])
-    lane = lax.broadcasted_iota(jnp.int32, (8, 128), 1)
-    sign = jnp.where(lane < 64, 1.0, -1.0)
-    place = lax.broadcasted_iota(jnp.int32, (8, NF), 1)
-    step = out_ref.shape[0]
-    first = pl.program_id(0) * step
-    energies = energy_ref[...]
-    for i in range(step):
-        tile = share_ref[first + i].astype(jnp.float32)
-        coef, parts = tile[:8], tile[8:]
-        facts = parts + pltpu.roll(parts, 125, 1) + pltpu.roll(parts, 122, 1)
-        rows16 = jnp.concatenate([coef * sign, pltpu.roll(coef, 64, 1)], axis=0)
-        image = jnp.dot(
-            rows16.astype(jnp.bfloat16), coeff_ref[first + i], preferred_element_type=jnp.float32
-        )
-        real, imag = image[:8], image[8:]
-        turn_real, turn_imag = facts[:, 0:1], facts[:, 1:2]
-        out_ref[i, :8] = (real * turn_real - imag * turn_imag) * inverse
-        out_ref[i, 8:] = (real * turn_imag + imag * turn_real) * inverse
-        energies = jnp.where(place == first + i, facts[:, 2:3], energies)
-    energy_ref[...] = energies
-
-
-def project(coeffs, shares, weights):
-    lanes = coeffs.shape[2]
-    step = 8
-    vmem = pl.BlockSpec(memory_space=pltpu.VMEM)
-    return pl.pallas_call(
-        project_kernel,
-        grid=(NF // step,),
-        out_shape=(
-            jax.ShapeDtypeStruct((NF, 2 * NM, lanes), jnp.float32),
-            jax.ShapeDtypeStruct((NM, NF), jnp.float32),
-        ),
-        in_specs=[vmem, vmem, pl.BlockSpec((1, lanes), lambda i: (0, 0))],
-        out_specs=(
-            pl.BlockSpec((step, 16, lanes), lambda i: (i, 0, 0)),
-            pl.BlockSpec((NM, NF), lambda i: (0, 0)),
-        ),
-        compiler_params=pltpu.CompilerParams(vmem_limit_bytes=6 << 20),
-        name="project",
-    )(coeffs, shares, weights)
-
-
 def shards(snapshots, weights, reference_field, start_basis):
     axes = ("grp", "row")
     devices, inner = lax.axis_size(axes), lax.axis_size("row")
     total_rows = snapshots.shape[1] * devices
     start = jnp.transpose(start_basis, (1, 2, 3, 0))
-    coeffs, shares = transform(
+    modes, energies = transform(
         total_rows, devices, inner,
         snapshots, jnp.asarray(pair_tables()), weights[None], reference_field[None], start,
     )
-    modes, energies = project(coeffs, shares, weights[None])
     return modes, energies.T
 
 

time: 57.8 us -> 58.1 us (level)
  local copies, waits for them, and re-layouts: 0.01 us -> 2.61 us
  Pallas kernels: 57 us -> 54.7 us
    pallas_call x1 -> x0, Pallas kernels: 5.43 us -> none  [project(): pl.pallas_call(project_kernel, grid=(NF // step,), out_shape=(jax.ShapeDt...]
    pallas_call x1, Pallas kernels: 51.6 us -> 54.7 us  [transform(): pl.pallas_call(functools.partial(transform_kernel, total_rows, devices, i...]
    unnamed x2, local copies, waits for them, and re-layouts: 0.01 us -> 2.61 us
where the time goes in v3:
time: 58.1 us; the launch traced here: 57.9 us
  Pallas kernels  54.7 us (94%)
  local copies, waits for them, and re-layouts  2.61 us (4%)
  between operations  0.64 us (1%)
    pallas_call x1, Pallas kernels, transform(): pl.pallas_call(functools.partial(transform_kernel, total_rows, devices, i...  54.7 us
    unnamed x2, local copies, waits for them, and re-layouts  2.61 us

profile of v3, /device:TPU:1, one launch (start us, length us, event | category | flops | bytes accessed | tf_op | source)
XLA Modules:
  0.0 57.9 jit_solution(4355819908091048988)
XLA Ops:
  0.6 54.7 %transform.1 = (f32[64,16,1024]{2,1,0:T(8,128)S(1)}, f32[8,64]{1,0:T(8,128)S(1)}) custom-call(bf16[8192,1024]{1,0:T(8,128)(2,1)} %snap_ref.1, bf16[8,256,384]{2,1,0:T(8,128)(2,1)} %constant.2.clone.table_hbm, f32[1,1024]{1,0:T(1,128)} %bitcast.6, f32[1,1024]{1,0:T(1,128)} %bitcast.7, f32[2,63,8,64]{3,2,1,0:T(8,128)} %bitcast.5), custom_call_target="tpu_custom_call" | custom-call | tf_op jit(solution)/shard_map/transform/pallas_call | solution.py:345
  55.3 2.0 %copy.9 = f32[64,16,1024]{2,1,0:T(8,128)} copy(f32[64,16,1024]{2,1,0:T(8,128)S(1)} %get-tuple-element.6) | data formatting | bytes 8388608
  57.4 0.6 %copy.10 = f32[64,8]{0,1:T(8,128)} copy(f32[64,8]{0,1:T(8,128)S(1)} %bitcast.4) | data formatting | bytes 4096

commit v4 on v3

--- a/solution.py
+++ b/solution.py
@@ -53,9 +53,9 @@
 def transform_kernel(
     total_rows, devices, inner,
     snap_ref, table_hbm, weight_hbm, field_hbm, start_hbm,
-    modes_ref, energy_ref,
-    coeff_ref, share_ref, buf, stage_a, stage_b, full_a, full_b, table_ref, weight_ref, field_ref, start_ref, gram_ref, pair_slots, slots,
-    snap_sems, side_sems, pair_sems, sum_send, sum_recv, share_send, share_recv,
+    coeff_ref, share_ref,
+    buf, stage_a, stage_b, full_a, full_b, table_ref, weight_ref, field_ref, start_ref, gram_ref, pair_slots, slots,
+    snap_sems, side_sems, pair_sems, sum_send, sum_recv, share_send, share_recv, relay_recv,
 ):
     pieces = 4
     piece_rows = snap_ref.shape[0] // pieces
@@ -243,22 +243,32 @@
         part = ref.at[pl.ds(0, count)]
         pltpu.make_async_copy(part, part, sem).wait()
 
-    def tile_came(f):
-        tile = share_ref.at[f]
-        pltpu.make_async_copy(tile, tile, share_recv.at[f]).wait()
-
     def near(d):
         return min(d, 4 - d)
 
-    def far_off(x, z, y):
-        return near(x) + near(z) + near(y)
+    peers = [(x, z, y) for x in range(4) for z in range(4) for y in range(4)][1:]
+    peers.sort(key=lambda p: -(near(p[0]) + near(p[1]) + near(p[2])))
+
+    def share(x, key, arrival):
+        pltpu.make_async_remote_copy(
+            src_ref=share_ref.at[mine],
+            dst_ref=share_ref.at[mine],
+            send_sem=share_send,
+            recv_sem=arrival,
+            device_id=(xs[x], rows_of[key]),
+            device_id_type=MESH,
+        ).start()
 
     @pl.when(jnp.logical_not(is_owner))
     def _():
         give(batches[last][1][-1]).start()
         all_of(gram_ref, NF, sum_send)
         side[3].wait()
-        tile_came(mine)
+        all_of(share_ref, 1, relay_recv)
+        for x, z, y in peers:
+            share(x, (z, y, 0), share_recv)
+        all_of(share_ref, NF - 1, share_recv)
+        all_of(share_ref, NF - 1, share_send)
 
     @pl.when(is_owner)
     def _():
@@ -276,49 +286,11 @@
         share_ref[mine] = solve_tile(packed, start, pad, total_rows)
         all_of(gram_ref, NF - 1, sum_send)
 
-        peers = [(x, key) for x in range(4) for key in rows_of if (x, key) != (0, (0, 0, 0))]
-        peers.sort(key=lambda p: -far_off(p[0], *p[1][:2]))
-        for x, key in peers:
-            pltpu.make_async_remote_copy(
-                src_ref=share_ref.at[mine],
-                dst_ref=share_ref.at[mine],
-                send_sem=share_send,
-                recv_sem=share_recv.at[mine],
-                device_id=(xs[x], rows_of[key]),
-                device_id_type=MESH,
-            ).start()
-
-    inverse_root = 1.0 / jnp.sqrt(weight_ref[...])
-    lane8 = lax.broadcasted_iota(jnp.int32, (8, 128), 1)
-    sign8 = jnp.where(lane8 < 64, 1.0, -1.0)
-    place = lax.broadcasted_iota(jnp.int32, (NM, NF), 1)
-    steps = [(x, z, y) for x in range(4) for z in range(4) for y in range(4)]
-    steps.sort(key=lambda p: far_off(*p))
-    energies = jnp.zeros((NM, NF), jnp.float32)
-    bounds = (0, 22, 42, 57, 64)
-    for low, high in zip(bounds[:-1], bounds[1:]):
-        fs = [xs[x] * 16 + zs[z] * 4 + ys[y] for x, z, y in steps[low:high]]
-        for f in fs[1:] if low == 0 else fs:
-            tile_came(f)
-        for f in fs:
-            tile = share_ref[f].astype(jnp.float32)
-            coef, parts = tile[:8], tile[8:]
-            facts = parts + pltpu.roll(parts, 125, 1) + pltpu.roll(parts, 122, 1)
-            rows16 = jnp.concatenate([coef * sign8, pltpu.roll(coef, 64, 1)], axis=0)
-            image = jnp.dot(
-                rows16.astype(jnp.bfloat16), coeff_ref[f], preferred_element_type=jnp.float32
-            )
-            real, imag = image[:8], image[8:]
-            turn_real, turn_imag = facts[:, 0:1], facts[:, 1:2]
-            modes_ref[f, :8] = (real * turn_real - imag * turn_imag) * inverse_root
-            modes_ref[f, 8:] = (real * turn_imag + imag * turn_real) * inverse_root
-            energies = jnp.where(place == f, facts[:, 2:3], energies)
-    energy_ref[...] = energies
-
-    @pl.when(is_owner)
-    def _():
-        for count in (NF, devices - 1 - NF):
-            all_of(share_ref, count, share_send)
+        share(0, (0, 0, 1), relay_recv)
+        for x, z, y in peers:
+            share(x, (z, y, 0), share_recv)
+        all_of(share_ref, NF - 1, share_recv)
+        all_of(share_ref, NF, share_send)
 
 
 def start_tile(start_ref, mine):
@@ -345,14 +317,12 @@
     return pl.pallas_call(
         functools.partial(transform_kernel, total_rows, devices, inner),
         out_shape=(
-            pltpu.VMEM((NF, 2 * NM, lanes), jnp.float32),
-            pltpu.VMEM((NM, NF), jnp.float32),
+            pltpu.VMEM((NF, 128, lanes), jnp.bfloat16),
+            pltpu.VMEM((NF, 16, 128), jnp.bfloat16),
         ),
         in_specs=[pl.BlockSpec(memory_space=pltpu.HBM)] * 5,
         out_specs=(vmem, vmem),
         scratch_shapes=[
-            pltpu.VMEM((NF, 128, lanes), jnp.bfloat16),
-            pltpu.VMEM((NF, 16, 128), jnp.bfloat16),
             pltpu.VMEM((2, rows + 128, XC), jnp.bfloat16),
             pltpu.VMEM((8, 256, XC), jnp.bfloat16),
             pltpu.VMEM((8, 256, XC), jnp.bfloat16),
@@ -371,10 +341,11 @@
             pltpu.SemaphoreType.DMA,
             pltpu.SemaphoreType.DMA,
             pltpu.SemaphoreType.DMA,
-            pltpu.SemaphoreType.DMA((NF,)),
+            pltpu.SemaphoreType.DMA,
+            pltpu.SemaphoreType.DMA,
         ],
         compiler_params=pltpu.CompilerParams(
-            vmem_limit_bytes=61200 * 1024, collective_id=0, has_side_effects=True
+            vmem_limit_bytes=48600 * 1024, collective_id=0, has_side_effects=True
         ),
         name="transform",
     )(snapshots, tables, weights, field, start)
@@ -502,15 +473,65 @@
     return jnp.concatenate([coef, facts], axis=0).astype(jnp.bfloat16)
 
 
+def project_kernel(coeff_ref, share_ref, weight_ref, out_ref, energy_ref, modes, sems):
+    inverse = 1.0 / jnp.sqrt(weight_ref[...])
+    lane = lax.broadcasted_iota(jnp.int32, (8, 128), 1)
+    sign = jnp.where(lane < 64, 1.0, -1.0)
+    place = lax.broadcasted_iota(jnp.int32, (NM, NF), 1)
+    energies = jnp.zeros((NM, NF), jnp.float32)
+    copies = []
+    for block in range(8):
+        span = slice(block * 8, block * 8 + 8)
+        for f in range(block * 8, block * 8 + 8):
+            tile = share_ref[f].astype(jnp.float32)
+            coef, parts = tile[:8], tile[8:]
+            facts = parts + pltpu.roll(parts, 125, 1) + pltpu.roll(parts, 122, 1)
+            rows16 = jnp.concatenate([coef * sign, pltpu.roll(coef, 64, 1)], axis=0)
+            image = jnp.dot(
+                rows16.astype(jnp.bfloat16), coeff_ref[f], preferred_element_type=jnp.float32
+            )
+            real, imag = image[:8], image[8:]
+            turn_real, turn_imag = facts[:, 0:1], facts[:, 1:2]
+            modes[f, :8] = (real * turn_real - imag * turn_imag) * inverse
+            modes[f, 8:] = (real * turn_imag + imag * turn_real) * inverse
+            energies = jnp.where(place == f, facts[:, 2:3], energies)
+        copies.append(pltpu.make_async_copy(modes.at[span], out_ref.at[span], sems.at[block]))
+        copies[-1].start()
+    energy_ref[...] = energies
+    for copy in copies:
+        copy.wait()
+
+
+def project(coeffs, shares, weights):
+    lanes = coeffs.shape[2]
+    vmem = pl.BlockSpec(memory_space=pltpu.VMEM)
+    return pl.pallas_call(
+        project_kernel,
+        out_shape=(
+            jax.ShapeDtypeStruct((NF, 2 * NM, lanes), jnp.float32),
+            jax.ShapeDtypeStruct((NM, NF), jnp.float32),
+        ),
+        in_specs=[vmem, vmem, vmem],
+        out_specs=(pl.BlockSpec(memory_space=pltpu.HBM), vmem),
+        scratch_shapes=[
+            pltpu.VMEM((NF, 2 * NM, lanes), jnp.float32),
+            pltpu.SemaphoreType.DMA((8,)),
+        ],
+        compiler_params=pltpu.CompilerParams(vmem_limit_bytes=12 << 20),
+        name="project",
+    )(coeffs, shares, weights)
+
+
 def shards(snapshots, weights, reference_field, start_basis):
     axes = ("grp", "row")
     devices, inner = lax.axis_size(axes), lax.axis_size("row")
     total_rows = snapshots.shape[1] * devices
     start = jnp.transpose(start_basis, (1, 2, 3, 0))
-    modes, energies = transform(
+    coeffs, shares = transform(
         total_rows, devices, inner,
         snapshots, jnp.asarray(pair_tables()), weights[None], reference_field[None], start,
     )
+    modes, energies = project(coeffs, shares, weights[None])
     return modes, energies.T
 
 

time: 58.1 us -> 57.4 us (0.988)
  local copies, waits for them, and re-layouts: 2.61 us -> 0.01 us
  Pallas kernels: 54.7 us -> 56.5 us
    pallas_call x0 -> x1, Pallas kernels: none -> 5.32 us  [project(): pl.pallas_call(project_kernel, out_shape=(jax.ShapeDtypeStruct((NF, 2 * N...]
    pallas_call x1, Pallas kernels: 54.7 us -> 51.1 us  [transform(): pl.pallas_call(functools.partial(transform_kernel, total_rows, devices, i...]
    unnamed x2, local copies, waits for them, and re-layouts: 2.61 us -> 0.01 us
where the time goes in v4:
time: 57.4 us; the launch traced here: 57.3 us
  Pallas kernels  56.5 us (98%)
  between operations  0.81 us (1%)
    pallas_call x1, Pallas kernels, transform(): pl.pallas_call(functools.partial(transform_kernel, total_rows, devices, i...  51.1 us
    pallas_call x1, Pallas kernels, project(): pl.pallas_call(project_kernel, out_shape=(jax.ShapeDtypeStruct((NF, 2 * N...  5.32 us

profile of v4, /device:TPU:1, one launch (start us, length us, event | category | flops | bytes accessed | tf_op | source)
XLA Modules:
  0.0 57.3 jit_solution(17147082058864666123)
XLA Ops:
  0.6 0.0 copy-start
  0.6 51.1 %transform.1 = (bf16[64,128,1024]{2,1,0:T(8,128)(2,1)S(1)}, bf16[64,16,128]{2,1,0:T(8,128)(2,1)S(1)}) custom-call(bf16[8192,1024]{1,0:T(8,128)(2,1)} %snap_ref.1, bf16[8,256,384]{2,1,0:T(8,128)(2,1)} %constant.2.clone.table_hbm, f32[1,1024]{1,0:T(1,128)} %bitcast.4, f32[1,1024]{1,0:T(1,128)} %bitcast.7, f32[2,63,8,64]{3,2,1,0:T(8,128)} %bitcast.6), custom_call_target="tpu_custom_call" | custom-call | tf_op jit(solution)/shard_map/transform/pallas_call | solution.py:317
  51.8 0.0 copy-done
  51.8 5.3 %project.1 = (f32[64,16,1024]{2,1,0:T(8,128)}, f32[8,64]{1,0:T(8,128)}) custom-call(bf16[64,128,1024]{2,1,0:T(8,128)(2,1)S(1)} %get-tuple-element.6.coeff_ref, bf16[64,16,128]{2,1,0:T(8,128)(2,1)S(1)} %get-tuple-element.7.share_ref, f32[1,1024]{1,0:T(1,128)S(1)} %bitcast.5), custom_call_target="tpu_custom_call" | custom-call | tf_op jit(solution)/shard_map/project/pallas_call | solution.py:508
Async XLA Ops:
  0.6 51.2 %copy-start = (f32[1024]{0:T(1024)S(1)}, f32[1024]{0:T(1024)}, u32[]{:S(2)}) copy-start(f32[1024]{0:T(1024)} %param.6) | copy-start | bytes 12292
